TPU v7x, 256 devices: a whole 4x4x8 slice. The times are simulated.
256 devices in a mesh: dp: 16 (over z, core), mp: 16 (over y, x).
Axes of the slice: x: 4, y: 4, z: 8, core: 2. Of those that a mesh axis runs over, the one named last changes fastest.
Arguments:
- candidates: bfloat16 [4096, 4096], P('dp', 'mp'), may hold values from -6 to 6
- hold_gate: bfloat16 [4096, 8192], P(None, 'mp'), may hold values from -0.09375 to 0.09375
- hold_up: bfloat16 [4096, 8192], P(None, 'mp'), may hold values from -0.09375 to 0.09375
- probe: float32 [8192], P('mp'), as said below
- chosen: int32 [16, 192], replicated, may hold values from 0 to 4095, as said below
- counts: int32 [16], replicated, may hold values from 24 to 192, as said below
- gate_w: bfloat16 [4096, 14336], P('dp', 'mp'), may hold values from -0.09375 to 0.09375
- up_w: bfloat16 [4096, 14336], P('dp', 'mp'), may hold values from -0.09375 to 0.09375
- cotangent: bfloat16 [3072, 14336], P('dp', 'mp'), may hold values from -6 to 6
Outputs:
- grad_gate: bfloat16 [4096, 14336], P('dp', 'mp')
- grad_up: bfloat16 [4096, 14336], P('dp', 'mp')
- hidden: bfloat16 [3072, 14336], P('dp', 'mp')
- cand_weight: float32 [4096], P('dp')
Inputs may be any that keep to these rules, and one draw needn't show every extreme that they name: `chosen`: all entries are distinct candidate indices. `counts`: exactly one training shard uses all 192 slots in every draw. `probe`: magnitudes at most 12 / sqrt(8192).
All inputs are finite; a program needn't handle non-finite values.
Results may differ from a plain program's by a relative error of at most 0.0057.
Values may be sent and summed in bfloat16 or wider, within the bound.
A program may use at most 128 MiB of HBM per device.

v0:
```python
import jax
import jax.numpy as jnp
from jax import lax
from jax.sharding import PartitionSpec as P


def gather_by_a2a(x, axis_name, axis):
    parts = lax.psum(1, axis_name)
    stacked = lax.all_to_all(
        jnp.broadcast_to(x[None], (parts,) + x.shape),
        axis_name,
        split_axis=0,
        concat_axis=0,
        tiled=True,
    )
    stacked = jnp.moveaxis(stacked, 0, axis)
    shape = list(x.shape)
    shape[axis] *= parts
    return stacked.reshape(shape)


def gather_rows(x):
    by_z = lax.all_gather(x, "z", axis=0)
    both = lax.all_gather(by_z, "core", axis=1)
    return both.reshape((-1,) + x.shape[1:])


def on_device(candidates, hold_gate, hold_up, probe, chosen, counts, gate_w, up_w, cotangent):
    cand_dev = candidates.shape[0]
    shards = chosen.shape[0]
    slots = chosen.shape[1]
    full_w = (gather_rows(gate_w), gather_rows(up_w))
    own_index = lax.axis_index("z") * lax.psum(1, "core") + lax.axis_index("core")
    source = chosen // cand_dev
    local_row = (chosen % cand_dev).reshape(-1)
    usable = (
        (jnp.arange(slots, dtype=jnp.int32)[None, :] < counts[:, None]) & (source == own_index)
    ).reshape(-1)
    onehot = (
        (local_row[:, None] == jnp.arange(cand_dev, dtype=jnp.int32)[None, :]) & usable[:, None]
    ).astype(jnp.bfloat16)
    picked = jnp.dot(onehot, candidates, preferred_element_type=jnp.float32).astype(jnp.bfloat16)
    picked = picked.reshape(shards, slots, candidates.shape[1])
    arrived = lax.all_to_all(picked, DP, split_axis=0, concat_axis=0, tiled=True)
    row_slab = jnp.sum(arrived.astype(jnp.float32), axis=0).astype(jnp.bfloat16)
    row_x = gather_by_a2a(row_slab, "mp", 1)
    row_slices = lax.all_to_all(row_x, DP, split_axis=1, concat_axis=0, tiled=True)
    incoming = gather_by_a2a(candidates, "mp", 1)
    hold_g = jnp.dot(incoming, hold_gate, preferred_element_type=jnp.float32)
    hold_u = jnp.dot(incoming, hold_up, preferred_element_type=jnp.float32)
    partial_score = jnp.sum(jax.nn.silu(hold_g) * hold_u * probe[None, :], axis=1)
    score = lax.psum(partial_score, "mp")
    cand_weight = jax.nn.sigmoid(score)
    picked_weight = (
        jnp.dot(
            onehot, cand_weight.astype(jnp.bfloat16)[:, None], preferred_element_type=jnp.float32
        )
        .astype(jnp.bfloat16)
        .reshape(shards, slots)
    )
    arrived_weight = lax.all_to_all(picked_weight, DP, split_axis=0, concat_axis=0, tiled=True)
    row_weight = jnp.sum(arrived_weight.astype(jnp.float32), axis=0)
    gate = jnp.dot(row_x, full_w[0], preferred_element_type=jnp.float32)
    up = jnp.dot(row_x, full_w[1], preferred_element_type=jnp.float32)
    hidden = (jax.nn.silu(gate) * up).astype(jnp.bfloat16)
    back = cotangent.astype(jnp.float32) * row_weight[:, None]
    sig = jax.nn.sigmoid(gate)
    d_up = (back * gate * sig).astype(jnp.bfloat16)
    d_gate = (back * up * sig * (1.0 + gate * (1.0 - sig))).astype(jnp.bfloat16)
    contract_rows = (((0,), (0,)), ((), ()))
    incoming = (gather_rows(d_gate), gather_rows(d_up))
    grad_g = lax.dot_general(
        row_slices, incoming[0], contract_rows, preferred_element_type=jnp.float32
    )
    grad_u = lax.dot_general(
        row_slices, incoming[1], contract_rows, preferred_element_type=jnp.float32
    )
    return (grad_g.astype(jnp.bfloat16), grad_u.astype(jnp.bfloat16), hidden, cand_weight)


DP = ("z", "core")


def solution(mesh):
    cores = 2
    mesh = jax.sharding.Mesh(
        mesh.devices.reshape(mesh.devices.shape[0] // cores, cores, mesh.devices.shape[1]),
        ("z", "core", "mp"),
    )
    placed = (
        P(DP, "mp"),
        P(None, "mp"),
        P(None, "mp"),
        P("mp"),
        P(),
        P(),
        P(DP, "mp"),
        P(DP, "mp"),
        P(DP, "mp"),
    )
    return jax.shard_map(
        on_device,
        mesh=mesh,
        in_specs=placed,
        out_specs=(P(DP, "mp"), P(DP, "mp"), P(DP, "mp"), P(DP)),
        check_vma=False,
    )
```

profile of v0, /device:TPU:1, one launch (start us, length us, event | category | flops | bytes accessed | tf_op | source)
XLA Modules:
  0.0 406.3 jit_solution(17809317110289626407)
XLA Ops:
  7.2 0.0 all-gather.21.cloned.1.call-start
  7.2 0.7 all-gather.21.cloned.1.call-update
  7.9 0.0 all-gather.17.cloned.1.call-start
  7.9 0.7 all-gather.17.cloned.1.call-update
  8.6 0.0 all-gather.23.cloned.1.call-start
  8.7 54.6 %all-gather.21.cloned.1.call-done = bf16[2048,896]{1,0:T(8,128)(2,1)} async-done(((bf16[256,896]{1,0:T(8,128)(2,1)}), bf16[2048,896]{1,0:T(8,128)(2,1)}) %all-gather.21.cloned.1.call-update) | async-done | bytes 3670032 | tf_op jit(solution)/shard_map/all_gather | solution.py:23
  63.3 0.0 copy-start.2
  63.3 0.0 all-gather.23.cloned.1.call-update
  63.3 0.0 all-gather.19.cloned.1.call-start
  63.3 50.2 %all-gather.17.cloned.1.call-done = bf16[2048,896]{1,0:T(8,128)(2,1)} async-done(((bf16[256,896]{1,0:T(8,128)(2,1)}), bf16[2048,896]{1,0:T(8,128)(2,1)}) %all-gather.17.cloned.1.call-update) | async-done | bytes 3670032 | tf_op jit(solution)/shard_map/all_gather | solution.py:23
  113.5 0.0 all-gather.19.cloned.1.call-update
  113.5 0.0 copy-done.2
  113.5 0.1 copy.16
  113.6 0.0 copy-start.3
  113.7 0.0 copy-start.4
  113.7 1.5 broadcast_in_dim.5
  115.2 6.5 %all-to-all-start.3 = ((bf16[16,256,256]{1,2,0:T(8,128)(2,1)}), bf16[16,256,256]{1,2,0:T(8,128)(2,1)S(1)}, u32[]{:S(2)}, u32[]{:S(2)}) async-start(bf16[16,256,256]{1,2,0:T(8,128)(2,1)} %broadcast_in_dim.5), calls=%async_computation.3 | async-start | bytes 4194304 | tf_op jit(solution)/shard_map/all_to_all | solution.py:9
  121.7 0.0 copy-done.3
  121.8 0.0 copy-done.4
  121.8 0.1 fusion.11
  121.8 0.1 and.28
  121.9 0.1 eq.23
  122.0 3.5 convolution_convert_fusion
  125.5 26.5 %all-to-all-done.3 = bf16[16,256,256]{1,2,0:T(8,128)(2,1)S(1)} async-done(((bf16[16,256,256]{1,2,0:T(8,128)(2,1)}), bf16[16,256,256]{1,2,0:T(8,128)(2,1)S(1)}, u32[]{:S(2)}, u32[]{:S(2)}) %all-to-all-start.3) | async-done | bytes 2097184 | tf_op jit(solution)/shard_map/all_to_all | solution.py:9
  152.0 0.0 copy-start
  152.0 1.3 copy-done
  153.3 6.6 %all-to-all-start = ((bf16[16,192,256]{2,1,0:T(8,128)(2,1)}), bf16[16,192,256]{2,1,0:T(8,128)(2,1)S(1)}, u32[]{:S(2)}, u32[]{:S(2)}) async-start(bf16[16,192,256]{2,1,0:T(8,128)(2,1)} %bitcast.41), calls=%async_computation | async-start | bytes 3145728 | tf_op jit(solution)/shard_map/all_to_all | solution.py:44
  159.9 0.0 copy-start.5
  159.9 0.0 copy-start.7
  159.9 4.3 %fusion.15 = f32[256,512]{1,0:T(8,128)S(1)} fusion(bf16[256,4096]{0,1:T(8,128)(2,1)} %bitcast.39, bf16[4096,512]{1,0:T(8,128)(2,1)} %param.10), kind=kOutput, calls=%fused_computation.32 | convolution fusion | flops 1073741824 | bytes 6815744 | tf_op jit(solution)/shard_map/dot_general | solution.py:49
  164.1 0.0 copy-done.1
  164.2 0.5 copy-done.5
  164.6 0.0 copy-done.7
  164.6 1.4 fusion.9
  166.0 31.8 %psum.7 = f32[256]{0:T(256)S(1)} all-reduce(f32[256]{0:T(256)S(1)} %fusion.9), channel_id=1, replica_groups=mesh['z'=8,'core'=2,'mp'=16] {'mp'}, use_global_device_ids=true, to_apply=%region_2.3 | all-reduce | flops 256 | bytes 2048 | tf_op jit(solution)/shard_map/psum | solution.py:52
  197.8 0.6 fusion.14
  198.4 2.5 fusion.1
  200.9 0.7 all_to_all.35
  201.6 0.0 all-to-all-done
  201.6 13.7 %all-to-all-start.4 = ((bf16[16,1,192]{2,1,0:T(2,128)(2,1)}), bf16[16,1,192]{2,1,0:T(2,128)(2,1)S(1)}, u32[]{:S(2)}, u32[]{:S(2)}) async-start(bf16[16,1,192]{2,1,0:T(2,128)(2,1)} %all_to_all.35), calls=%async_computation.4 | async-start | bytes 32768 | tf_op jit(solution)/shard_map/all_to_all | solution.py:61
  215.4 0.2 reduce_sum.30
  215.6 7.1 %all-to-all-done.4 = bf16[16,1,192]{2,1,0:T(2,128)(2,1)S(1)} async-done(((bf16[16,1,192]{2,1,0:T(2,128)(2,1)}), bf16[16,1,192]{2,1,0:T(2,128)(2,1)S(1)}, u32[]{:S(2)}, u32[]{:S(2)}) %all-to-all-start.4) | async-done | bytes 6176 | tf_op jit(solution)/shard_map/all_to_all | solution.py:61
  222.7 1.3 broadcast_in_dim.4
  224.0 3.7 all-to-all-start.1
  227.8 0.0 all-gather.29.cloned.1.call-start
  227.8 24.8 %all-to-all-done.1 = bf16[16,192,256]{2,1,0:T(8,128)(2,1)S(1)} async-done(((bf16[16,192,256]{2,1,0:T(8,128)(2,1)}), bf16[16,192,256]{2,1,0:T(8,128)(2,1)S(1)}, u32[]{:S(2)}, u32[]{:S(2)}) %all-to-all-start.1) | async-done | bytes 1572896 | tf_op jit(solution)/shard_map/all_to_all | solution.py:9
  252.7 0.2 copy.19
  252.8 0.0 all-gather.23.cloned.1.call-done
  252.9 0.0 copy-start.6
  252.9 5.8 %fusion.16 = f32[192,896]{1,0:T(8,128)} fusion(bf16[192,4096]{1,0:T(8,128)(2,1)S(1)} %bitcast.42, bf16[4096,896]{1,0:T(8,128)(2,1)} %bitcast.47), kind=kOutput, calls=%fused_computation.33 | convolution fusion | flops 1409286144 | bytes 9601024 | tf_op jit(solution)/shard_map/dot_general | solution.py:63
  258.7 0.0 copy-done.6
  258.7 6.1 %multiply_convert_fusion = (bf16[192,896]{1,0:T(8,128)(2,1)}, bf16[192,896]{1,0:T(8,128)(2,1)}, bf16[192,896]{1,0:T(8,128)(2,1)}) fusion(f32[192,896]{1,0:T(8,128)} %fusion.16, f32[192]{0:T(256)S(1)} %convert_reduce_fusion, bf16[192,896]{1,0:T(8,128)(2,1)S(1)} %copy-done.6, bf16[192,4096]{1,0:T(8,128)(2,1)S(1)} %bitcast.43, bf16[4096,896]{1,0:T(8,128)(2,1)} %bitcast.48), kind=kOutput, calls=%fused_computation.13 | convolution fusion | flops 1412382720 | bytes 10978048 | tf_op jit(solution)/shard_map/dot_general | solution.py:64
  264.9 0.0 all-gather.29.cloned.1.call-update
  264.9 0.0 all-gather.25.cloned.1.call-start
  264.9 0.5 all-gather.25.cloned.1.call-update
  265.5 0.0 all-gather.31.cloned.1.call-start
  265.5 32.7 %all-gather.29.cloned.1.call-done = bf16[1536,896]{1,0:T(8,128)(2,1)} async-done(((bf16[192,896]{1,0:T(8,128)(2,1)}), bf16[1536,896]{1,0:T(8,128)(2,1)}) %all-gather.29.cloned.1.call-update) | async-done | bytes 2752528 | tf_op jit(solution)/shard_map/all_gather | solution.py:23
  298.2 0.0 all-gather.31.cloned.1.call-update
  298.3 0.0 all-gather.27.cloned.1.call-start
  298.3 43.6 %all-gather.25.cloned.1.call-done = bf16[1536,896]{1,0:T(8,128)(2,1)} async-done(((bf16[192,896]{1,0:T(8,128)(2,1)}), bf16[1536,896]{1,0:T(8,128)(2,1)}) %all-gather.25.cloned.1.call-update) | async-done | bytes 2752528 | tf_op jit(solution)/shard_map/all_gather | solution.py:23
  341.9 0.0 all-gather.27.cloned.1.call-update
  341.9 47.2 %all_to_all.41 = bf16[192,16,256]{2,0,1:T(8,128)(2,1)S(1)} all-to-all(bf16[192,16,256]{2,0,1:T(8,128)(2,1)S(1)} %bitcast.34), channel_id=1, replica_groups=mesh['z'=8,'core'=2,'mp'=16] {'z','core'}, dimensions={1} | all-to-all | bytes 3145728 | tf_op jit(solution)/shard_map/all_to_all | solution.py:47
  389.1 5.2 %convolution_convert_fusion.1 = bf16[256,896]{1,0:T(8,128)(2,1)} fusion(bf16[3072,256]{1,0:T(8,128)(2,1)S(1)} %bitcast.44, bf16[3072,896]{1,0:T(8,128)(2,1)} %bitcast.49), kind=kOutput, calls=%fused_computation.8 | convolution fusion | flops 1409515520 | bytes 7536640 | tf_op jit(solution)/shard_map/dot_general | solution.py:75
  394.3 5.2 %convolution_convert_fusion.2 = bf16[256,896]{1,0:T(8,128)(2,1)} fusion(bf16[3072,256]{1,0:T(8,128)(2,1)S(1)} %bitcast.45, bf16[3072,896]{1,0:T(8,128)(2,1)} %bitcast.50), kind=kOutput, calls=%fused_computation.9 | convolution fusion | flops 1409515520 | bytes 7536640 | tf_op jit(solution)/shard_map/dot_general | solution.py:72
  (8 shorter events, 0.1 us)
Async XLA Ops:
  7.2 56.1 %all-gather.21.cloned.1.call-start = ((), (), s32[]{:S(2)}) async-start(), calls=%async_computation.7 | async-start | bytes 4128768 | tf_op jit(solution)/shard_map/all_gather | solution.py:23
  7.9 105.6 %all-gather.17.cloned.1.call-start = ((), (), s32[]{:S(2)}) async-start(), calls=%async_computation.5 | async-start | bytes 4128768 | tf_op jit(solution)/shard_map/all_gather | solution.py:23
  8.6 244.2 %all-gather.23.cloned.1.call-start = ((), (), s32[]{:S(2)}) async-start(), calls=%async_computation.8 | async-start | bytes 11010048 | tf_op jit(solution)/shard_map/all_gather | solution.py:24
  63.3 50.3 %copy-start.2 = (bf16[256,256]{1,0:T(8,128)(2,1)S(1)}, bf16[256,256]{1,0:T(8,128)(2,1)}, u32[]{:S(2)}) copy-start(bf16[256,256]{1,0:T(8,128)(2,1)} %param.9) | copy-start | bytes 393220
  63.3 195.5 %all-gather.19.cloned.1.call-start = ((), (), s32[]{:S(2)}) async-start(), calls=%async_computation.6 | async-start | bytes 11010048 | tf_op jit(solution)/shard_map/all_gather | solution.py:24
  113.6 8.1 %copy-start.3 = (s32[16,192]{1,0:T(8,128)S(1)}, s32[16,192]{1,0:T(8,128)}, u32[]{:S(2)}) copy-start(s32[16,192]{1,0:T(8,128)} %param.13) | copy-start | bytes 36868
  113.7 8.1 %copy-start.4 = (s32[16]{0:T(128)S(1)}, s32[16]{0:T(128)}, u32[]{:S(2)}) copy-start(s32[16]{0:T(128)} %param.14) | copy-start | bytes 196
  115.2 36.8 %all-to-all-start.3 = ((bf16[16,256,256]{1,2,0:T(8,128)(2,1)}), bf16[16,256,256]{1,2,0:T(8,128)(2,1)S(1)}, u32[]{:S(2)}, u32[]{:S(2)}) async-start(bf16[16,256,256]{1,2,0:T(8,128)(2,1)} %broadcast_in_dim.5), calls=%async_computation.3 | async-start | bytes 4194304 | tf_op jit(solution)/shard_map/all_to_all | solution.py:9
  152.0 1.3 copy-start
  153.3 48.3 %all-to-all-start = ((bf16[16,192,256]{2,1,0:T(8,128)(2,1)}), bf16[16,192,256]{2,1,0:T(8,128)(2,1)S(1)}, u32[]{:S(2)}, u32[]{:S(2)}) async-start(bf16[16,192,256]{2,1,0:T(8,128)(2,1)} %bitcast.41), calls=%async_computation | async-start | bytes 3145728 | tf_op jit(solution)/shard_map/all_to_all | solution.py:44
  159.9 4.3 %copy-start.1 = (bf16[16,256,256]{1,2,0:T(8,128)(2,1)S(1)}, bf16[16,256,256]{1,2,0:T(8,128)(2,1)}, u32[]{:S(2)}) copy-start(bf16[16,256,256]{1,2,0:T(8,128)(2,1)} %copy-done) | copy-start | bytes 6291460
  159.9 4.8 %copy-start.5 = (bf16[4096,512]{1,0:T(8,128)(2,1)S(1)}, bf16[4096,512]{1,0:T(8,128)(2,1)}, u32[]{:S(2)}) copy-start(bf16[4096,512]{1,0:T(8,128)(2,1)} %param.11) | copy-start | bytes 12582916
  159.9 4.8 %copy-start.7 = (f32[512]{0:T(512)S(1)}, f32[512]{0:T(512)}, u32[]{:S(2)}) copy-start(f32[512]{0:T(512)} %param.12) | copy-start | bytes 6148
  201.6 21.1 %all-to-all-start.4 = ((bf16[16,1,192]{2,1,0:T(2,128)(2,1)}), bf16[16,1,192]{2,1,0:T(2,128)(2,1)S(1)}, u32[]{:S(2)}, u32[]{:S(2)}) async-start(bf16[16,1,192]{2,1,0:T(2,128)(2,1)} %all_to_all.35), calls=%async_computation.4 | async-start | bytes 32768 | tf_op jit(solution)/shard_map/all_to_all | solution.py:61
  224.0 28.6 %all-to-all-start.1 = ((bf16[16,192,256]{2,1,0:T(8,128)(2,1)}), bf16[16,192,256]{2,1,0:T(8,128)(2,1)S(1)}, u32[]{:S(2)}, u32[]{:S(2)}) async-start(bf16[16,192,256]{2,1,0:T(8,128)(2,1)} %broadcast_in_dim.4), calls=%async_computation.1 | async-start | bytes 3145728 | tf_op jit(solution)/shard_map/all_to_all | solution.py:9
  227.8 70.5 %all-gather.29.cloned.1.call-start = ((), (), s32[]{:S(2)}) async-start(), calls=%async_computation.11 | async-start | bytes 3096576 | tf_op jit(solution)/shard_map/all_gather | solution.py:23
  252.9 5.9 %copy-start.6 = (bf16[192,896]{1,0:T(8,128)(2,1)S(1)}, bf16[192,896]{1,0:T(8,128)(2,1)}, u32[]{:S(2)}) copy-start(bf16[192,896]{1,0:T(8,128)(2,1)} %param.17) | copy-start | bytes 1032196
  264.9 77.0 %all-gather.25.cloned.1.call-start = ((), (), s32[]{:S(2)}) async-start(), calls=%async_computation.9 | async-start | bytes 3096576 | tf_op jit(solution)/shard_map/all_gather | solution.py:23
  265.5 123.6 %all-gather.31.cloned.1.call-start = ((), (), s32[]{:S(2)}) async-start(), calls=%async_computation.12 | async-start | bytes 8257536 | tf_op jit(solution)/shard_map/all_gather | solution.py:24
  298.3 96.0 %all-gather.27.cloned.1.call-start = ((), (), s32[]{:S(2)}) async-start(), calls=%async_computation.10 | async-start | bytes 8257536 | tf_op jit(solution)/shard_map/all_gather | solution.py:24
Sparse Core Ops, SparseCore 0:
  9.8 53.4 all-gather.20
  65.0 48.4 all-gather.16
  115.3 23.1 all-gather.22
  140.1 25.0 all-gather.18
  265.0 33.1 all-gather.28
  300.4 41.3 all-gather.24
  343.6 23.0 all-gather.30
  368.5 22.2 all-gather.26
where the time goes:
time: 407 us; the launch traced here: 406 us
  waiting for transfers between devices  241 us (59%)
  blocking collectives  79.1 us (19%)
  matrix products  33.9 us (8%)
  starting transfers between devices  30.9 us (8%)
  between operations  14.3 us (4%)
  local copies, waits for them, and re-layouts  5.83 us (1%)
    all_gather x4, waiting for transfers between devices, gather_rows(): by_z = lax.all_gather(x, 'z', axis=0)  181 us
    all_to_all x2, waiting for transfers between devices, gather_by_a2a(): lax.all_to_all(jnp.broadcast_to(x[None], (parts,) + x.shape), axis_name,...  51.3 us
    all_to_all x1, blocking collectives, on_device(): lax.all_to_all(row_x, DP, split_axis=1, concat_axis=0, tiled=True)  47.2 us
    psum x1, blocking collectives, on_device(): score = lax.psum(partial_score, 'mp')  31.8 us
    all_to_all x1, starting transfers between devices, on_device(): lax.all_to_all(picked_weight, DP, split_axis=0, concat_axis=0, tiled=True)  13.7 us
    all_to_all x2, starting transfers between devices, gather_by_a2a(): lax.all_to_all(jnp.broadcast_to(x[None], (parts,) + x.shape), axis_name,...  10.2 us
  transfers between devices with their start and end apart: 12, of which 7 were waited for; matrix products, arithmetic and copies ran while one was open for 7% of the time, Pallas kernels for 0%

commit v1 on v0

--- a/solution.py
+++ b/solution.py
@@ -49,7 +49,7 @@
     hold_g = jnp.dot(incoming, hold_gate, preferred_element_type=jnp.float32)
     hold_u = jnp.dot(incoming, hold_up, preferred_element_type=jnp.float32)
     partial_score = jnp.sum(jax.nn.silu(hold_g) * hold_u * probe[None, :], axis=1)
-    score = lax.psum(partial_score, "mp")
+    score = jnp.sum(lax.all_gather(partial_score, "mp"), axis=0)
     cand_weight = jax.nn.sigmoid(score)
     picked_weight = (
         jnp.dot(

time: 407 us -> 394 us (0.968)
  blocking collectives: 79.1 us -> 66.4 us
  waiting for transfers between devices: 241 us -> 251 us
  starting transfers between devices: 30.9 us -> 21.2 us
    psum x1 -> x0, blocking collectives: 31.8 us -> none  [on_device(): score = lax.psum(partial_score, 'mp')]
    all_gather x0 -> x1, blocking collectives: none -> 19.1 us  [on_device(): score = jnp.sum(lax.all_gather(partial_score, 'mp'), axis=0)]
    all_to_all x1, starting transfers between devices: 13.7 us -> 4.14 us  [on_device(): lax.all_to_all(picked_weight, DP, split_axis=0, concat_axis=0, tiled=True)]
    all_to_all x1, waiting for transfers between devices: 0.01 us -> 9.41 us  [on_device(): lax.all_to_all(picked, DP, split_axis=0, concat_axis=0, tiled=True)]
  transfers between devices with their start and end apart: 12 -> 12, of which waited for: 7 -> 8; matrix products, arithmetic and copies ran while one was open for 7% -> 7% of each run, Pallas kernels for 0% -> 0%
where the time goes in v1:
time: 394 us; the launch traced here: 393 us
  waiting for transfers between devices  251 us (64%)
  blocking collectives  66.4 us (17%)
  matrix products  33.9 us (9%)
  starting transfers between devices  21.2 us (5%)
  between operations  14.3 us (4%)
  local copies, waits for them, and re-layouts  5.83 us (1%)
    all_gather x4, waiting for transfers between devices, gather_rows(): by_z = lax.all_gather(x, 'z', axis=0)  181 us
    all_to_all x2, waiting for transfers between devices, gather_by_a2a(): lax.all_to_all(jnp.broadcast_to(x[None], (parts,) + x.shape), axis_name,...  51.3 us
    all_to_all x1, blocking collectives, on_device(): lax.all_to_all(row_x, DP, split_axis=1, concat_axis=0, tiled=True)  47.2 us
    all_gather x1, blocking collectives, on_device(): score = jnp.sum(lax.all_gather(partial_score, 'mp'), axis=0)  19.1 us
    all_to_all x2, starting transfers between devices, gather_by_a2a(): lax.all_to_all(jnp.broadcast_to(x[None], (parts,) + x.shape), axis_name,...  10.2 us
    all_to_all x1, waiting for transfers between devices, on_device(): lax.all_to_all(picked, DP, split_axis=0, concat_axis=0, tiled=True)  9.41 us
  transfers between devices with their start and end apart: 12, of which 8 were waited for; matrix products, arithmetic and copies ran while one was open for 7% of the time, Pallas kernels for 0%

profile of v1, /device:TPU:1, one launch (start us, length us, event | category | flops | bytes accessed | tf_op | source)
XLA Modules:
  0.0 393.4 jit_solution(1177093022415134326)
XLA Ops:
  7.2 0.0 all-gather.23.cloned.1.call-start
  7.2 0.7 all-gather.23.cloned.1.call-update
  7.9 0.0 all-gather.19.cloned.1.call-start
  7.9 0.7 all-gather.19.cloned.1.call-update
  8.6 0.0 all-gather.25.cloned.1.call-start
  8.7 54.6 %all-gather.23.cloned.1.call-done = bf16[2048,896]{1,0:T(8,128)(2,1)} async-done(((bf16[256,896]{1,0:T(8,128)(2,1)}), bf16[2048,896]{1,0:T(8,128)(2,1)}) %all-gather.23.cloned.1.call-update) | async-done | bytes 3670032 | tf_op jit(solution)/shard_map/all_gather | solution.py:23
  63.3 0.0 copy-start.2
  63.3 0.0 all-gather.25.cloned.1.call-update
  63.3 0.0 all-gather.21.cloned.1.call-start
  63.3 50.2 %all-gather.19.cloned.1.call-done = bf16[2048,896]{1,0:T(8,128)(2,1)} async-done(((bf16[256,896]{1,0:T(8,128)(2,1)}), bf16[2048,896]{1,0:T(8,128)(2,1)}) %all-gather.19.cloned.1.call-update) | async-done | bytes 3670032 | tf_op jit(solution)/shard_map/all_gather | solution.py:23
  113.5 0.0 all-gather.21.cloned.1.call-update
  113.5 0.0 copy-done.2
  113.5 0.1 copy.16
  113.6 0.0 copy-start.3
  113.7 0.0 copy-start.4
  113.7 1.5 broadcast_in_dim.5
  115.2 6.5 %all-to-all-start.3 = ((bf16[16,256,256]{1,2,0:T(8,128)(2,1)}), bf16[16,256,256]{1,2,0:T(8,128)(2,1)S(1)}, u32[]{:S(2)}, u32[]{:S(2)}) async-start(bf16[16,256,256]{1,2,0:T(8,128)(2,1)} %broadcast_in_dim.5), calls=%async_computation.3 | async-start | bytes 4194304 | tf_op jit(solution)/shard_map/all_to_all | solution.py:9
  121.7 0.0 copy-done.3
  121.8 0.0 copy-done.4
  121.8 0.1 fusion.11
  121.8 0.1 and.28
  121.9 0.1 eq.23
  122.0 3.5 convolution_convert_fusion
  125.5 26.5 %all-to-all-done.3 = bf16[16,256,256]{1,2,0:T(8,128)(2,1)S(1)} async-done(((bf16[16,256,256]{1,2,0:T(8,128)(2,1)}), bf16[16,256,256]{1,2,0:T(8,128)(2,1)S(1)}, u32[]{:S(2)}, u32[]{:S(2)}) %all-to-all-start.3) | async-done | bytes 2097184 | tf_op jit(solution)/shard_map/all_to_all | solution.py:9
  152.0 0.0 copy-start
  152.0 1.3 copy-done
  153.3 6.6 %all-to-all-start = ((bf16[16,192,256]{2,1,0:T(8,128)(2,1)}), bf16[16,192,256]{2,1,0:T(8,128)(2,1)S(1)}, u32[]{:S(2)}, u32[]{:S(2)}) async-start(bf16[16,192,256]{2,1,0:T(8,128)(2,1)} %bitcast.42), calls=%async_computation | async-start | bytes 3145728 | tf_op jit(solution)/shard_map/all_to_all | solution.py:44
  159.9 0.0 copy-start.5
  159.9 0.0 copy-start.7
  159.9 4.3 %fusion.15 = f32[256,512]{1,0:T(8,128)S(1)} fusion(bf16[256,4096]{0,1:T(8,128)(2,1)} %bitcast.40, bf16[4096,512]{1,0:T(8,128)(2,1)} %param.10), kind=kOutput, calls=%fused_computation.32 | convolution fusion | flops 1073741824 | bytes 6815744 | tf_op jit(solution)/shard_map/dot_general | solution.py:49
  164.1 0.0 copy-done.1
  164.2 0.5 copy-done.5
  164.6 0.0 copy-done.7
  164.6 1.4 fusion.9
  166.0 19.1 %all-gather.9 = f32[16,1,256]{2,1,0:T(1,128)S(1)} all-gather(f32[1,1,256]{2,1,0:T(1,128)S(1)} %bitcast.48), channel_id=2, replica_groups=mesh['z'=8,'core'=2,'mp'=16] {'mp'}, dimensions={0}, use_global_device_ids=true | all-gather | bytes 17408 | tf_op jit(solution)/shard_map/all_gather | solution.py:52
  185.2 0.6 fusion.14
  185.8 2.5 fusion.1
  188.3 0.7 all_to_all.35
  189.0 9.4 %all-to-all-done = bf16[16,192,256]{2,1,0:T(8,128)(2,1)S(1)} async-done(((bf16[16,192,256]{2,1,0:T(8,128)(2,1)}), bf16[16,192,256]{2,1,0:T(8,128)(2,1)S(1)}, u32[]{:S(2)}, u32[]{:S(2)}) %all-to-all-start) | async-done | bytes 1572896 | tf_op jit(solution)/shard_map/all_to_all | solution.py:44
  198.4 4.1 %all-to-all-start.4 = ((bf16[16,1,192]{2,1,0:T(2,128)(2,1)}), bf16[16,1,192]{2,1,0:T(2,128)(2,1)S(1)}, u32[]{:S(2)}, u32[]{:S(2)}) async-start(bf16[16,1,192]{2,1,0:T(2,128)(2,1)} %all_to_all.35), calls=%async_computation.4 | async-start | bytes 32768 | tf_op jit(solution)/shard_map/all_to_all | solution.py:61
  202.5 0.2 reduce_sum.39
  202.7 7.1 %all-to-all-done.4 = bf16[16,1,192]{2,1,0:T(2,128)(2,1)S(1)} async-done(((bf16[16,1,192]{2,1,0:T(2,128)(2,1)}), bf16[16,1,192]{2,1,0:T(2,128)(2,1)S(1)}, u32[]{:S(2)}, u32[]{:S(2)}) %all-to-all-start.4) | async-done | bytes 6176 | tf_op jit(solution)/shard_map/all_to_all | solution.py:61
  209.8 1.3 broadcast_in_dim.4
  211.2 3.7 all-to-all-start.1
  214.9 0.0 all-gather.31.cloned.1.call-start
  215.0 24.8 %all-to-all-done.1 = bf16[16,192,256]{2,1,0:T(8,128)(2,1)S(1)} async-done(((bf16[16,192,256]{2,1,0:T(8,128)(2,1)}), bf16[16,192,256]{2,1,0:T(8,128)(2,1)S(1)}, u32[]{:S(2)}, u32[]{:S(2)}) %all-to-all-start.1) | async-done | bytes 1572896 | tf_op jit(solution)/shard_map/all_to_all | solution.py:9
  239.8 0.2 copy.19
  240.0 0.0 all-gather.25.cloned.1.call-done
  240.0 0.0 copy-start.6
  240.0 5.8 %fusion.16 = f32[192,896]{1,0:T(8,128)} fusion(bf16[192,4096]{1,0:T(8,128)(2,1)S(1)} %bitcast.43, bf16[4096,896]{1,0:T(8,128)(2,1)} %bitcast.49), kind=kOutput, calls=%fused_computation.33 | convolution fusion | flops 1409286144 | bytes 9601024 | tf_op jit(solution)/shard_map/dot_general | solution.py:63
  245.9 0.0 copy-done.6
  245.9 6.1 %multiply_convert_fusion = (bf16[192,896]{1,0:T(8,128)(2,1)}, bf16[192,896]{1,0:T(8,128)(2,1)}, bf16[192,896]{1,0:T(8,128)(2,1)}) fusion(f32[192,896]{1,0:T(8,128)} %fusion.16, f32[192]{0:T(256)S(1)} %convert_reduce_fusion, bf16[192,896]{1,0:T(8,128)(2,1)S(1)} %copy-done.6, bf16[192,4096]{1,0:T(8,128)(2,1)S(1)} %bitcast.44, bf16[4096,896]{1,0:T(8,128)(2,1)} %bitcast.50), kind=kOutput, calls=%fused_computation.13 | convolution fusion | flops 1412382720 | bytes 10978048 | tf_op jit(solution)/shard_map/dot_general | solution.py:64
  252.0 0.0 all-gather.31.cloned.1.call-update
  252.0 0.0 all-gather.27.cloned.1.call-start
  252.1 0.5 all-gather.27.cloned.1.call-update
  252.6 0.0 all-gather.33.cloned.1.call-start
  252.7 32.7 %all-gather.31.cloned.1.call-done = bf16[1536,896]{1,0:T(8,128)(2,1)} async-done(((bf16[192,896]{1,0:T(8,128)(2,1)}), bf16[1536,896]{1,0:T(8,128)(2,1)}) %all-gather.31.cloned.1.call-update) | async-done | bytes 2752528 | tf_op jit(solution)/shard_map/all_gather | solution.py:23
  285.4 0.0 all-gather.33.cloned.1.call-update
  285.4 0.0 all-gather.29.cloned.1.call-start
  285.4 43.6 %all-gather.27.cloned.1.call-done = bf16[1536,896]{1,0:T(8,128)(2,1)} async-done(((bf16[192,896]{1,0:T(8,128)(2,1)}), bf16[1536,896]{1,0:T(8,128)(2,1)}) %all-gather.27.cloned.1.call-update) | async-done | bytes 2752528 | tf_op jit(solution)/shard_map/all_gather | solution.py:23
  329.0 0.0 all-gather.29.cloned.1.call-update
  329.0 47.2 %all_to_all.41 = bf16[192,16,256]{2,0,1:T(8,128)(2,1)S(1)} all-to-all(bf16[192,16,256]{2,0,1:T(8,128)(2,1)S(1)} %bitcast.35), channel_id=1, replica_groups=mesh['z'=8,'core'=2,'mp'=16] {'z','core'}, dimensions={1} | all-to-all | bytes 3145728 | tf_op jit(solution)/shard_map/all_to_all | solution.py:47
  376.2 5.2 %convolution_convert_fusion.1 = bf16[256,896]{1,0:T(8,128)(2,1)} fusion(bf16[3072,256]{1,0:T(8,128)(2,1)S(1)} %bitcast.45, bf16[3072,896]{1,0:T(8,128)(2,1)} %bitcast.51), kind=kOutput, calls=%fused_computation.8 | convolution fusion | flops 1409515520 | bytes 7536640 | tf_op jit(solution)/shard_map/dot_general | solution.py:75
  381.4 5.2 %convolution_convert_fusion.2 = bf16[256,896]{1,0:T(8,128)(2,1)} fusion(bf16[3072,256]{1,0:T(8,128)(2,1)S(1)} %bitcast.46, bf16[3072,896]{1,0:T(8,128)(2,1)} %bitcast.52), kind=kOutput, calls=%fused_computation.9 | convolution fusion | flops 1409515520 | bytes 7536640 | tf_op jit(solution)/shard_map/dot_general | solution.py:72
  (9 shorter events, 0.1 us)
Async XLA Ops:
  7.2 56.1 %all-gather.23.cloned.1.call-start = ((), (), s32[]{:S(2)}) async-start(), calls=%async_computation.7 | async-start | bytes 4128768 | tf_op jit(solution)/shard_map/all_gather | solution.py:23
  7.9 105.6 %all-gather.19.cloned.1.call-start = ((), (), s32[]{:S(2)}) async-start(), calls=%async_computation.5 | async-start | bytes 4128768 | tf_op jit(solution)/shard_map/all_gather | solution.py:23
  8.6 231.4 %all-gather.25.cloned.1.call-start = ((), (), s32[]{:S(2)}) async-start(), calls=%async_computation.8 | async-start | bytes 11010048 | tf_op jit(solution)/shard_map/all_gather | solution.py:24
  63.3 50.3 %copy-start.2 = (bf16[256,256]{1,0:T(8,128)(2,1)S(1)}, bf16[256,256]{1,0:T(8,128)(2,1)}, u32[]{:S(2)}) copy-start(bf16[256,256]{1,0:T(8,128)(2,1)} %param.9) | copy-start | bytes 393220
  63.3 182.6 %all-gather.21.cloned.1.call-start = ((), (), s32[]{:S(2)}) async-start(), calls=%async_computation.6 | async-start | bytes 11010048 | tf_op jit(solution)/shard_map/all_gather | solution.py:24
  113.6 8.1 %copy-start.3 = (s32[16,192]{1,0:T(8,128)S(1)}, s32[16,192]{1,0:T(8,128)}, u32[]{:S(2)}) copy-start(s32[16,192]{1,0:T(8,128)} %param.13) | copy-start | bytes 36868
  113.7 8.1 %copy-start.4 = (s32[16]{0:T(128)S(1)}, s32[16]{0:T(128)}, u32[]{:S(2)}) copy-start(s32[16]{0:T(128)} %param.14) | copy-start | bytes 196
  115.2 36.8 %all-to-all-start.3 = ((bf16[16,256,256]{1,2,0:T(8,128)(2,1)}), bf16[16,256,256]{1,2,0:T(8,128)(2,1)S(1)}, u32[]{:S(2)}, u32[]{:S(2)}) async-start(bf16[16,256,256]{1,2,0:T(8,128)(2,1)} %broadcast_in_dim.5), calls=%async_computation.3 | async-start | bytes 4194304 | tf_op jit(solution)/shard_map/all_to_all | solution.py:9
  152.0 1.3 copy-start
  153.3 45.1 %all-to-all-start = ((bf16[16,192,256]{2,1,0:T(8,128)(2,1)}), bf16[16,192,256]{2,1,0:T(8,128)(2,1)S(1)}, u32[]{:S(2)}, u32[]{:S(2)}) async-start(bf16[16,192,256]{2,1,0:T(8,128)(2,1)} %bitcast.42), calls=%async_computation | async-start | bytes 3145728 | tf_op jit(solution)/shard_map/all_to_all | solution.py:44
  159.9 4.3 %copy-start.1 = (bf16[16,256,256]{1,2,0:T(8,128)(2,1)S(1)}, bf16[16,256,256]{1,2,0:T(8,128)(2,1)}, u32[]{:S(2)}) copy-start(bf16[16,256,256]{1,2,0:T(8,128)(2,1)} %copy-done) | copy-start | bytes 6291460
  159.9 4.8 %copy-start.5 = (bf16[4096,512]{1,0:T(8,128)(2,1)S(1)}, bf16[4096,512]{1,0:T(8,128)(2,1)}, u32[]{:S(2)}) copy-start(bf16[4096,512]{1,0:T(8,128)(2,1)} %param.11) | copy-start | bytes 12582916
  159.9 4.8 %copy-start.7 = (f32[512]{0:T(512)S(1)}, f32[512]{0:T(512)}, u32[]{:S(2)}) copy-start(f32[512]{0:T(512)} %param.12) | copy-start | bytes 6148
  198.4 11.5 %all-to-all-start.4 = ((bf16[16,1,192]{2,1,0:T(2,128)(2,1)}), bf16[16,1,192]{2,1,0:T(2,128)(2,1)S(1)}, u32[]{:S(2)}, u32[]{:S(2)}) async-start(bf16[16,1,192]{2,1,0:T(2,128)(2,1)} %all_to_all.35), calls=%async_computation.4 | async-start | bytes 32768 | tf_op jit(solution)/shard_map/all_to_all | solution.py:61
  211.2 28.6 %all-to-all-start.1 = ((bf16[16,192,256]{2,1,0:T(8,128)(2,1)}), bf16[16,192,256]{2,1,0:T(8,128)(2,1)S(1)}, u32[]{:S(2)}, u32[]{:S(2)}) async-start(bf16[16,192,256]{2,1,0:T(8,128)(2,1)} %broadcast_in_dim.4), calls=%async_computation.1 | async-start | bytes 3145728 | tf_op jit(solution)/shard_map/all_to_all | solution.py:9
  214.9 70.5 %all-gather.31.cloned.1.call-start = ((), (), s32[]{:S(2)}) async-start(), calls=%async_computation.11 | async-start | bytes 3096576 | tf_op jit(solution)/shard_map/all_gather | solution.py:23
  240.0 5.9 %copy-start.6 = (bf16[192,896]{1,0:T(8,128)(2,1)S(1)}, bf16[192,896]{1,0:T(8,128)(2,1)}, u32[]{:S(2)}) copy-start(bf16[192,896]{1,0:T(8,128)(2,1)} %param.17) | copy-start | bytes 1032196
  252.0 76.9 %all-gather.27.cloned.1.call-start = ((), (), s32[]{:S(2)}) async-start(), calls=%async_computation.9 | async-start | bytes 3096576 | tf_op jit(solution)/shard_map/all_gather | solution.py:23
  252.6 123.6 %all-gather.33.cloned.1.call-start = ((), (), s32[]{:S(2)}) async-start(), calls=%async_computation.12 | async-start | bytes 8257536 | tf_op jit(solution)/shard_map/all_gather | solution.py:24
  285.4 96.0 %all-gather.29.cloned.1.call-start = ((), (), s32[]{:S(2)}) async-start(), calls=%async_computation.10 | async-start | bytes 8257536 | tf_op jit(solution)/shard_map/all_gather | solution.py:24
Sparse Core Ops, SparseCore 0:
  9.8 53.4 all-gather.22
  65.0 48.4 all-gather.18
  115.3 23.1 all-gather.24
  140.1 25.0 all-gather.20
  252.2 33.1 all-gather.30
  287.6 41.3 all-gather.26
  330.8 23.0 all-gather.32
  355.6 22.2 all-gather.28
